TPU v7x, 32 devices: a whole 2x2x4 slice. The times are simulated.
32 devices in a mesh: grp: 2 (over y), prow: 4 (over z), pcol: 4 (over x, core).
Axes of the slice: x: 2, y: 2, z: 4, core: 2. Of those that a mesh axis runs over, the one named last changes fastest.
Arguments:
- eigvecs: float32 [8192, 4096], P(('grp', 'prow'), 'pcol'), parts along dimension 0, may hold values from -6 to 6
- y_panels: float32 [2, 8192, 256], P(None, ('grp', 'prow'), 'pcol'), parts along dimension 1, as said below
- t_factors: float32 [4, 256, 256], P('grp'), parts along dimension 0, as said below
Outputs:
- result: float32 [8192, 4096], P(('grp', 'prow'), 'pcol'), parts along dimension 0
There are 2 independent parts, one for each index of `grp`. A program takes and returns all parts, laid end to end along the dimension named above; each array names one. Nothing has to cross between parts.
Inputs may be any that keep to these rules, and one draw needn't show every extreme that they name: `y_panels`: column j of panel k is zero in rows above k * 256 + j and one in that row; t_factors[k] is upper triangular with diagonal between 0.5 and 1.5. Each t_factors[k] is upper triangular.
All inputs are finite; a program needn't handle non-finite values.
Results may differ from a plain program's by a relative error of at most 0.0001.
Values sent between devices are 32-bit elements; how exact they have to be, the bound alone decides.
No kernel may reach another device: no remote copies, remote signals or barrier semaphores. Data moves between devices by JAX's collectives and lax.ppermute only.
A program may use at most 64 MiB of HBM per device.

v0:
```python
import jax
import jax.numpy as jnp
from jax import lax
from jax.sharding import PartitionSpec as P


def update(current, vectors, triangle):
    highest = lax.Precision.HIGHEST
    local_sums = jnp.einsum("rc,rk->ck", current, vectors, precision=highest)
    sums = lax.psum(local_sums, "prow")
    scaled = jnp.einsum("ck,jk->cj", sums, triangle, precision=highest)
    return current - jnp.einsum("rj,cj->rc", vectors, scaled, precision=highest)


def per_device(eigvecs, y_panels, t_factors):
    gathered = lax.all_gather(y_panels, "pcol", axis=2, tiled=True)
    count = gathered.shape[0]
    current = eigvecs
    for index in reversed(range(count)):
        current = update(current, gathered[index], t_factors[index])
    return current


def solution(mesh):
    return jax.shard_map(
        per_device,
        mesh=mesh,
        in_specs=(
            P(("grp", "prow"), "pcol"),
            P(None, ("grp", "prow"), "pcol"),
            P("grp", None, None),
        ),
        out_specs=P(("grp", "prow"), "pcol"),
        check_vma=False,
    )
```

profile of v0, /device:TPU:0, one launch (start us, length us, event | category | flops | bytes accessed | tf_op | source)
XLA Modules:
  0.0 183.0 jit_solution(13575742015813939483)
XLA Ops:
  6.5 0.0 all-gather.2.cloned.1.call-start
  6.5 0.7 all-gather.2.cloned.1.call-update
  7.3 0.0 all-reduce.3.cloned.1.call-start
  7.3 26.9 %all-gather.2.cloned.1.call-done = f32[2,1024,256]{1,2,0:T(8,128)} async-done(((f32[2,1024,64]{1,2,0:T(8,128)}), f32[2,1024,256]{1,2,0:T(8,128)}) %all-gather.2.cloned.1.call-update) | async-done | bytes 2097168 | tf_op jit(solution)/shard_map/all_gather | solution.py:16
  34.2 10.1 %fusion = f32[1024,256]{1,0:T(8,128)} fusion(f32[1024,1024]{1,0:T(8,128)} %param.3, f32[2,1024,256]{1,2,0:T(8,128)} %all-gather.2.cloned.1.call-done), kind=kOutput, calls=%fused_computation.4 | convolution fusion | flops 3221225472 | bytes 6291456 | tf_op jit(solution)/shard_map/rc,rk->ck/dot_general | solution.py:9
  44.3 0.0 all-reduce.3.cloned.1.call-update
  44.4 0.0 copy-start.2
  44.4 0.0 copy-start.1
  44.4 0.2 all-reduce.5.cloned.1.call-start
  44.6 5.5 %copy.4 = f32[1024,1024]{0,1:T(8,128)} copy(f32[1024,1024]{1,0:T(8,128)} %param.3) | data formatting | bytes 8388608 | tf_op args[0]
  50.1 46.3 %all-reduce.3.cloned.1.call-done = f32[1024,256]{1,0:T(8,128)} async-done(((f32[1024,256]{1,0:T(8,128)}), f32[1024,256]{1,0:T(8,128)}) %all-reduce.3.cloned.1.call-update) | async-done | bytes 1048592 | tf_op jit(solution)/shard_map/psum | solution.py:10
  96.4 0.0 copy-done.2
  96.4 2.3 %fusion.4 = f32[1024,256]{1,0:T(8,128)S(1)} fusion(f32[1024,256]{1,0:T(8,128)} %all-reduce.3.cloned.1.call-done, f32[2,256,256]{2,1,0:T(8,128)S(1)} %copy-done.2), kind=kOutput, calls=%fused_computation.8 | convolution fusion | flops 805306368 | bytes 2359296 | tf_op jit(solution)/shard_map/ck,jk->cj/dot_general | solution.py:11
  98.7 0.0 copy-done.1
  98.7 5.7 %bitcast_subtract_fusion.1 = f32[1024,1024]{0,1:T(8,128)S(1)} fusion(f32[1024,1024]{0,1:T(8,128)} %copy.4, f32[1024,256]{1,0:T(8,128)S(1)} %fusion.4, f32[2,1024,256]{1,2,0:T(8,128)S(1)} %copy-done.1), kind=kOutput, calls=%fused_computation.1 | convolution fusion | flops 3222274048 | bytes 10485760 | tf_op jit(solution)/shard_map/rj,cj->rc/dot_general | solution.py:12
  104.4 0.0 copy-start
  104.4 2.0 %copy-done = f32[1024,1024]{0,1:T(8,128)} copy-done((f32[1024,1024]{0,1:T(8,128)}, f32[1024,1024]{0,1:T(8,128)S(1)}, u32[]{:S(2)}) %copy-start) | copy-done | bytes 4194328
  106.4 4.5 %fusion.1 = f32[1024,256]{1,0:T(8,128)} fusion(f32[1024,1024]{0,1:T(8,128)S(1)} %bitcast_subtract_fusion.1, f32[2,1024,256]{1,2,0:T(8,128)S(1)} %copy-done.1), kind=kOutput, calls=%fused_computation.5 | convolution fusion | flops 3221225472 | bytes 6291456 | tf_op jit(solution)/shard_map/rc,rk->ck/dot_general | solution.py:9
  110.9 0.0 all-reduce.5.cloned.1.call-update
  110.9 51.3 %all-reduce.5.cloned.1.call-done = f32[1024,256]{1,0:T(8,128)} async-done(((f32[1024,256]{1,0:T(8,128)}), f32[1024,256]{1,0:T(8,128)}) %all-reduce.5.cloned.1.call-update) | async-done | bytes 1048592 | tf_op jit(solution)/shard_map/psum | solution.py:10
  162.3 2.3 %fusion.2 = f32[1024,256]{1,0:T(8,128)S(1)} fusion(f32[1024,256]{1,0:T(8,128)} %all-reduce.5.cloned.1.call-done, f32[2,256,256]{2,1,0:T(8,128)S(1)} %copy-done.2), kind=kOutput, calls=%fused_computation.6 | convolution fusion | flops 805306368 | bytes 2359296 | tf_op jit(solution)/shard_map/ck,jk->cj/dot_general | solution.py:11
  164.5 6.6 %bitcast_subtract_fusion = f32[1024,1024]{0,1:T(8,128)} fusion(f32[1024,1024]{0,1:T(8,128)} %copy-done, f32[1024,256]{1,0:T(8,128)S(1)} %fusion.2, f32[2,1024,256]{1,2,0:T(8,128)S(1)} %copy-done.1), kind=kOutput, calls=%fused_computation | convolution fusion | flops 3222274048 | bytes 10485760 | tf_op jit(solution)/shard_map/rj,cj->rc/dot_general | solution.py:12
  171.1 5.3 %copy.5 = f32[1024,1024]{1,0:T(8,128)} copy(f32[1024,1024]{0,1:T(8,128)} %bitcast_subtract_fusion) | data formatting | bytes 8388608 | tf_op jit(solution)/shard_map/sub | solution.py:12
Async XLA Ops:
  6.5 27.7 %all-gather.2.cloned.1.call-start = ((), (), s32[]{:S(2)}) async-start(), calls=%async_computation | async-start | bytes 2621440 | tf_op jit(solution)/shard_map/all_gather | solution.py:16
  7.3 89.2 %all-reduce.3.cloned.1.call-start = ((), (), s32[]{:S(2)}) async-start(), calls=%async_computation.1 | async-start | bytes 2097152 | tf_op jit(solution)/shard_map/psum | solution.py:10
  44.4 52.1 %copy-start.2 = (f32[2,256,256]{2,1,0:T(8,128)S(1)}, f32[2,256,256]{2,1,0:T(8,128)}, u32[]{:S(2)}) copy-start(f32[2,256,256]{2,1,0:T(8,128)} %param.5) | copy-start | bytes 1572868
  44.4 54.3 %copy-start.1 = (f32[2,1024,256]{1,2,0:T(8,128)S(1)}, f32[2,1024,256]{1,2,0:T(8,128)}, u32[]{:S(2)}) copy-start(f32[2,1024,256]{1,2,0:T(8,128)} %all-gather.2.cloned.1.call-done) | copy-start | bytes 6291460
  44.4 117.9 %all-reduce.5.cloned.1.call-start = ((), (), s32[]{:S(2)}) async-start(), calls=%async_computation.2 | async-start | bytes 2097152 | tf_op jit(solution)/shard_map/psum | solution.py:10
  104.4 2.0 %copy-start = (f32[1024,1024]{0,1:T(8,128)}, f32[1024,1024]{0,1:T(8,128)S(1)}, u32[]{:S(2)}) copy-start(f32[1024,1024]{0,1:T(8,128)S(1)} %bitcast_subtract_fusion.1) | copy-start | bytes 12582916
Sparse Core Ops, SparseCore 0:
  8.9 25.2 all-gather.1
  44.5 51.8 all-reduce.2
  111.1 51.1 all-reduce.4
where the time goes:
time: 183 us
  waiting for transfers between devices  125 us (68%)
  matrix products  31.5 us (17%)
  between operations  13.2 us (7%)
  local copies, waits for them, and re-layouts  12.8 us (7%)
    psum x2, waiting for transfers between devices, update(): sums = lax.psum(local_sums, 'prow')  97.6 us
    all_gather x1, waiting for transfers between devices, per_device(): gathered = lax.all_gather(y_panels, 'pcol', axis=2, tiled=True)  26.9 us
    dot_general x2, matrix products, update(): local_sums = jnp.einsum('rc,rk->ck', current, vectors, precision=highest)  14.6 us
    dot_general x2, matrix products, update(): return current - jnp.einsum('rj,cj->rc', vectors, scaled, precision=highest)  12.3 us
    unnamed x7, local copies, waits for them, and re-layouts  7.5 us
    sub x1, local copies, waits for them, and re-layouts, update(): return current - jnp.einsum('rj,cj->rc', vectors, scaled, precision=highest)  5.34 us
    dot_general x2, matrix products, update(): scaled = jnp.einsum('ck,jk->cj', sums, triangle, precision=highest)  4.51 us
  transfers between devices with their start and end apart: 3, of which 3 were waited for; matrix products, arithmetic and copies ran while one was open for 3% of the time, Pallas kernels for 0%

commit v1 on v0

--- a/solution.py
+++ b/solution.py
@@ -4,10 +4,15 @@
 from jax.sharding import PartitionSpec as P
 
 
+def add_all(x, name):
+    parts = lax.all_gather(x, name)
+    return jnp.sum(parts, axis=0)
+
+
 def update(current, vectors, triangle):
     highest = lax.Precision.HIGHEST
     local_sums = jnp.einsum("rc,rk->ck", current, vectors, precision=highest)
-    sums = lax.psum(local_sums, "prow")
+    sums = add_all(local_sums, "prow")
     scaled = jnp.einsum("ck,jk->cj", sums, triangle, precision=highest)
     return current - jnp.einsum("rj,cj->rc", vectors, scaled, precision=highest)
 

time: 183 us -> 245 us (1.34)
  waiting for transfers between devices: 125 us -> 182 us
  other arithmetic: 0 us -> 5.19 us
    all_gather x0 -> x2, waiting for transfers between devices: none -> 155 us  [add_all(): parts = lax.all_gather(x, name)]
    psum x2 -> x0, waiting for transfers between devices: 97.6 us -> none  [update(): sums = lax.psum(local_sums, 'prow')]
    reduce_sum x0 -> x2, other arithmetic: none -> 5.19 us  [add_all(): return jnp.sum(parts, axis=0)]
    unnamed x7 -> x5, local copies, waits for them, and re-layouts: 7.5 us -> 7.36 us
  transfers between devices with their start and end apart: 3 -> 3, of which waited for: 3 -> 3; matrix products, arithmetic and copies ran while one was open for 3% -> 2% of each run, Pallas kernels for 0% -> 0%
where the time goes in v1:
time: 245 us
  waiting for transfers between devices  182 us (74%)
  matrix products  30.9 us (13%)
  between operations  13.2 us (5%)
  local copies, waits for them, and re-layouts  12.7 us (5%)
  other arithmetic  5.19 us (2%)
    all_gather x2, waiting for transfers between devices, add_all(): parts = lax.all_gather(x, name)  155 us
    all_gather x1, waiting for transfers between devices, per_device(): gathered = lax.all_gather(y_panels, 'pcol', axis=2, tiled=True)  26.9 us
    dot_general x2, matrix products, update(): local_sums = jnp.einsum('rc,rk->ck', current, vectors, precision=highest)  14.6 us
    dot_general x2, matrix products, update(): return current - jnp.einsum('rj,cj->rc', vectors, scaled, precision=highest)  12.3 us
    unnamed x5, local copies, waits for them, and re-layouts  7.36 us
    sub x1, local copies, waits for them, and re-layouts, update(): return current - jnp.einsum('rj,cj->rc', vectors, scaled, precision=highest)  5.34 us
    reduce_sum x2, other arithmetic, add_all(): return jnp.sum(parts, axis=0)  5.19 us
  transfers between devices with their start and end apart: 3, of which 3 were waited for; matrix products, arithmetic and copies ran while one was open for 2% of the time, Pallas kernels for 0%

profile of v1, /device:TPU:0, one launch (start us, length us, event | category | flops | bytes accessed | tf_op | source)
XLA Modules:
  0.0 244.5 jit_solution(6343151451239452119)
XLA Ops:
  6.5 0.0 all-gather.6.cloned.1.call-start
  6.5 0.7 all-gather.6.cloned.1.call-update
  7.3 0.0 all-gather.8.cloned.1.call-start
  7.3 26.9 %all-gather.6.cloned.1.call-done = f32[2,1024,256]{1,2,0:T(8,128)} async-done(((f32[2,1024,64]{1,2,0:T(8,128)}), f32[2,1024,256]{1,2,0:T(8,128)}) %all-gather.6.cloned.1.call-update) | async-done | bytes 2097168 | tf_op jit(solution)/shard_map/all_gather | solution.py:21
  34.2 10.1 %fusion = f32[1024,256]{1,0:T(8,128)} fusion(f32[1024,1024]{1,0:T(8,128)} %param.3, f32[2,1024,256]{1,2,0:T(8,128)} %all-gather.6.cloned.1.call-done), kind=kOutput, calls=%fused_computation.4 | convolution fusion | flops 3221225472 | bytes 6291456 | tf_op jit(solution)/shard_map/rc,rk->ck/dot_general | solution.py:14
  44.3 0.0 all-gather.8.cloned.1.call-update
  44.4 0.2 all-gather.10.cloned.1.call-start
  44.6 5.3 %copy.4 = f32[1024,1024]{0,1:T(8,128)} copy(f32[1024,1024]{1,0:T(8,128)} %param.3) | data formatting | bytes 8388608 | tf_op args[0]
  50.0 0.0 copy-start.1
  50.0 75.3 %all-gather.8.cloned.1.call-done = f32[4096,256]{1,0:T(8,128)} async-done(((f32[1024,256]{1,0:T(8,128)}), f32[4096,256]{1,0:T(8,128)}) %all-gather.8.cloned.1.call-update) | async-done | bytes 4194320 | tf_op jit(solution)/shard_map/all_gather | solution.py:8
  125.3 2.6 %reduce_sum.18 = f32[1024,256]{1,0:T(8,128)S(1)} reduce(f32[4,1024,256]{2,1,0:T(8,128)} %bitcast.26, f32[]{:T(128)} %constant.0.clone.1), dimensions={0}, to_apply=%region_0.0 | reduce | flops 786432 | bytes 5242884 | tf_op jit(solution)/shard_map/reduce_sum | solution.py:9
  127.9 2.0 fusion.4
  129.9 0.0 copy-done.1
  129.9 5.7 %bitcast_subtract_fusion.1 = f32[1024,1024]{0,1:T(8,128)S(1)} fusion(f32[1024,1024]{0,1:T(8,128)} %copy.4, f32[1024,256]{1,0:T(8,128)S(1)} %fusion.4, f32[2,1024,256]{1,2,0:T(8,128)S(1)} %copy-done.1), kind=kOutput, calls=%fused_computation.1 | convolution fusion | flops 3222274048 | bytes 10485760 | tf_op jit(solution)/shard_map/rj,cj->rc/dot_general | solution.py:17
  135.6 0.0 copy-start
  135.6 2.0 copy-done
  137.6 4.4 %fusion.1 = f32[1024,256]{1,0:T(8,128)} fusion(f32[1024,1024]{0,1:T(8,128)S(1)} %bitcast_subtract_fusion.1, f32[2,1024,256]{1,2,0:T(8,128)S(1)} %copy-done.1), kind=kOutput, calls=%fused_computation.5 | convolution fusion | flops 3221225472 | bytes 6291456 | tf_op jit(solution)/shard_map/rc,rk->ck/dot_general | solution.py:14
  142.0 0.0 all-gather.10.cloned.1.call-update
  142.0 79.4 %all-gather.10.cloned.1.call-done = f32[4096,256]{1,0:T(8,128)} async-done(((f32[1024,256]{1,0:T(8,128)}), f32[4096,256]{1,0:T(8,128)}) %all-gather.10.cloned.1.call-update) | async-done | bytes 4194320 | tf_op jit(solution)/shard_map/all_gather | solution.py:8
  221.4 2.6 %reduce_sum.19 = f32[1024,256]{1,0:T(8,128)S(1)} reduce(f32[4,1024,256]{2,1,0:T(8,128)} %bitcast.27, f32[]{:T(128)} %constant.0.clone.1), dimensions={0}, to_apply=%region_1.0 | reduce | flops 786432 | bytes 5242884 | tf_op jit(solution)/shard_map/reduce_sum | solution.py:9
  224.0 2.0 fusion.2
  226.0 6.6 %bitcast_subtract_fusion = f32[1024,1024]{0,1:T(8,128)} fusion(f32[1024,1024]{0,1:T(8,128)} %copy-done, f32[1024,256]{1,0:T(8,128)S(1)} %fusion.2, f32[2,1024,256]{1,2,0:T(8,128)S(1)} %copy-done.1), kind=kOutput, calls=%fused_computation | convolution fusion | flops 3222274048 | bytes 10485760 | tf_op jit(solution)/shard_map/rj,cj->rc/dot_general | solution.py:17
  232.6 5.3 %copy.5 = f32[1024,1024]{1,0:T(8,128)} copy(f32[1024,1024]{0,1:T(8,128)} %bitcast_subtract_fusion) | data formatting | bytes 8388608 | tf_op jit(solution)/shard_map/sub | solution.py:17
Async XLA Ops:
  6.5 27.7 %all-gather.6.cloned.1.call-start = ((), (), s32[]{:S(2)}) async-start(), calls=%async_computation | async-start | bytes 2621440 | tf_op jit(solution)/shard_map/all_gather | solution.py:21
  7.3 118.0 %all-gather.8.cloned.1.call-start = ((), (), s32[]{:S(2)}) async-start(), calls=%async_computation.1 | async-start | bytes 5242880 | tf_op jit(solution)/shard_map/all_gather | solution.py:8
  44.4 177.1 %all-gather.10.cloned.1.call-start = ((), (), s32[]{:S(2)}) async-start(), calls=%async_computation.2 | async-start | bytes 5242880 | tf_op jit(solution)/shard_map/all_gather | solution.py:8
  50.0 79.9 %copy-start.1 = (f32[2,1024,256]{1,2,0:T(8,128)S(1)}, f32[2,1024,256]{1,2,0:T(8,128)}, u32[]{:S(2)}) copy-start(f32[2,1024,256]{1,2,0:T(8,128)} %all-gather.6.cloned.1.call-done) | copy-start | bytes 6291460
  135.6 2.0 copy-start
Sparse Core Ops, SparseCore 0:
  8.9 25.2 all-gather.5
  44.5 80.7 all-gather.7
  142.2 79.2 all-gather.9
